TPU v7x, 128 devices: a whole 4x4x4 slice. The times are simulated.
128 devices in a mesh: prow: 16 (over x, z), pcol: 8 (over y, core).
Axes of the slice: x: 4, y: 4, z: 4, core: 2. Of those that a mesh axis runs over, the one named last changes fastest.
Arguments:
- rhs: float32 [31, 64, 2048], P(None, None, 'prow'), may hold values from -6 to 6
- factor: bfloat16 [98, 2048, 2048], P(None, 'prow', 'pcol'), may hold values from -0.03125 to 0.03125
- inverse: bfloat16 [31, 2048, 2048], P(None, 'pcol', 'prow')
- pattern: int32 [98], replicated, may hold values 0 or 1
Outputs:
- solution: float32 [31, 64, 2048], P(None, None, 'prow')
- forward_solution: float32 [31, 64, 2048], P(None, None, 'pcol')
All inputs are finite; a program needn't handle non-finite values.
Results may differ from a plain program's by a relative error of at most 0.011.
Values sent between devices are 32-bit elements; how exact they have to be, the bound alone decides.
No kernel may reach another device: no remote copies, remote signals or barrier semaphores. Data moves between devices by JAX's collectives and lax.ppermute only.
A program may use at most 64 MiB of HBM per device.

v0:
```python
import jax
import jax.numpy as jnp
from jax import lax
from jax.sharding import PartitionSpec as P

LEV = 5


def block_start(tree_depth):
    return (tree_depth - 2) * 2**tree_depth + 2


def sum_columns(values):
    result = lax.psum(values, "pcol")
    return lax.optimization_barrier(result)


def sum_rows(values):
    result = lax.psum(values, "prow")
    return lax.optimization_barrier(result)


def per_device(rhs, factor, inverse, pattern):
    live = pattern.astype(jnp.float32)
    partial_value = jnp.zeros(rhs.shape, jnp.float32)
    forward_levels = [None] * LEV
    for tree_depth in range(LEV - 1, -1, -1):
        first = 2**tree_depth - 1
        count = 2**tree_depth
        residual = rhs[first : first + count]
        if tree_depth < LEV - 1:
            residual = residual - sum_columns(partial_value[first : first + count])
        rounded = residual.astype(jnp.bfloat16)
        pieces = jnp.einsum(
            "nrc,nwc->nrw",
            rounded,
            inverse[first : first + count],
            preferred_element_type=jnp.float32,
        )
        forward = sum_rows(pieces)
        forward_levels[tree_depth] = forward
        narrow = forward.astype(jnp.bfloat16)
        if tree_depth > 0:
            start = block_start(tree_depth)
            weights = live[start : start + count * tree_depth].reshape(count, tree_depth)
            for upward in range(1, tree_depth + 1):
                blocks = factor[start + upward - 1 : start + count * tree_depth : tree_depth]
                terms = jnp.einsum(
                    "nrc,nwc->nrw", narrow, blocks, preferred_element_type=jnp.float32
                )
                terms = terms * weights[:, upward - 1][:, None, None]
                groups = count >> upward
                terms = terms.reshape((groups, 2**upward) + terms.shape[1:]).sum(axis=1)
                target = 2 ** (tree_depth - upward) - 1
                partial_value = partial_value.at[target : target + groups].add(terms)
    solved = [None] * LEV
    solved_narrow = [None] * LEV
    for tree_depth in range(LEV):
        first = 2**tree_depth - 1
        count = 2**tree_depth
        target_vec = forward_levels[tree_depth]
        if tree_depth > 0:
            start = block_start(tree_depth)
            weights = live[start : start + count * tree_depth].reshape(count, tree_depth)
            gathered = jnp.zeros(target_vec.shape, jnp.float32)
            for upward in range(1, tree_depth + 1):
                blocks = factor[start + upward - 1 : start + count * tree_depth : tree_depth]
                above = jnp.repeat(solved_narrow[tree_depth - upward], 2**upward, axis=0)
                terms = jnp.einsum(
                    "nrw,nwc->nrc", above, blocks, preferred_element_type=jnp.float32
                )
                gathered = gathered + terms * weights[:, upward - 1][:, None, None]
            target_vec = target_vec - sum_rows(gathered)
        rounded = target_vec.astype(jnp.bfloat16)
        pieces = jnp.einsum(
            "nrw,nwc->nrc",
            rounded,
            inverse[first : first + count],
            preferred_element_type=jnp.float32,
        )
        solution = sum_columns(pieces)
        solved[tree_depth] = solution
        solved_narrow[tree_depth] = solution.astype(jnp.bfloat16)
    return (jnp.concatenate(solved, axis=0), jnp.concatenate(forward_levels, axis=0))


def solution(mesh):
    in_specs = (P(None, None, "prow"), P(None, "prow", "pcol"), P(None, "pcol", "prow"), P())
    out_specs = (P(None, None, "prow"), P(None, None, "pcol"))
    return jax.shard_map(
        per_device, mesh=mesh, in_specs=in_specs, out_specs=out_specs, check_vma=False
    )
```

profile of v0, /device:TPU:0, one launch (start us, length us, event | category | flops | bytes accessed | tf_op | source)
XLA Modules:
  0.0 1293.9 jit_solution(4972876091253898043)
XLA Ops:
  7.2 2.8 fusion.20
  10.5 90.9 %all-reduce.18.cloned.1.call-done = f32[16,64,256]{2,1,0:T(8,128)} async-done(((f32[16,64,256]{2,1,0:T(8,128)}), f32[16,64,256]{2,1,0:T(8,128)}) %all-reduce.18.cloned.1.call-update) | async-done | bytes 1048592 | tf_op jit(solution)/shard_map/psum | solution.py:19
  102.8 1.7 bitcast_reduce_fusion.2
  104.5 1.7 bitcast_reduce_fusion.1
  110.6 59.1 %all-reduce.20.cloned.1.call-done = f32[8,64,128]{2,1,0:T(8,128)} async-done(((f32[8,64,128]{2,1,0:T(8,128)}), f32[8,64,128]{2,1,0:T(8,128)}) %all-reduce.20.cloned.1.call-update) | async-done | bytes 262160 | tf_op jit(solution)/shard_map/psum | solution.py:14
  169.8 2.3 fusion.31
  172.5 85.8 %all-reduce.22.cloned.1.call-done = f32[8,64,256]{2,1,0:T(8,128)} async-done(((f32[8,64,256]{2,1,0:T(8,128)}), f32[8,64,256]{2,1,0:T(8,128)}) %all-reduce.22.cloned.1.call-update) | async-done | bytes 524304 | tf_op jit(solution)/shard_map/psum | solution.py:19
  262.3 58.7 %all-reduce.24.cloned.1.call-done = f32[4,64,128]{2,1,0:T(8,128)} async-done(((f32[4,64,128]{2,1,0:T(8,128)}), f32[4,64,128]{2,1,0:T(8,128)}) %all-reduce.24.cloned.1.call-update) | async-done | bytes 131088 | tf_op jit(solution)/shard_map/psum | solution.py:14
  321.0 2.0 fusion.45
  323.4 84.9 %all-reduce.26.cloned.1.call-done = f32[4,64,256]{2,1,0:T(8,128)} async-done(((f32[4,64,256]{2,1,0:T(8,128)}), f32[4,64,256]{2,1,0:T(8,128)}) %all-reduce.26.cloned.1.call-update) | async-done | bytes 262160 | tf_op jit(solution)/shard_map/psum | solution.py:19
  411.7 57.4 %all-reduce.28.cloned.1.call-done = f32[2,64,128]{2,1,0:T(8,128)} async-done(((f32[2,64,128]{2,1,0:T(8,128)}), f32[2,64,128]{2,1,0:T(8,128)}) %all-reduce.28.cloned.1.call-update) | async-done | bytes 65552 | tf_op jit(solution)/shard_map/psum | solution.py:14
  469.1 1.8 fusion.57
  472.2 82.4 %all-reduce.30.cloned.1.call-done = f32[2,64,256]{2,1,0:T(8,128)} async-done(((f32[2,64,256]{2,1,0:T(8,128)}), f32[2,64,256]{2,1,0:T(8,128)}) %all-reduce.30.cloned.1.call-update) | async-done | bytes 131088 | tf_op jit(solution)/shard_map/psum | solution.py:19
  555.7 24.1 %psum.133 = f32[1,64,128]{2,1,0:T(8,128)S(1)} all-reduce(f32[1,64,128]{2,1,0:T(8,128)S(1)} %fusion.71), channel_id=1, replica_groups=mesh['prow'=16,'pcol'=8] {'pcol'}, use_global_device_ids=true, to_apply=%region_17.0 | all-reduce | flops 8192 | bytes 65536 | tf_op jit(solution)/shard_map/psum | solution.py:14
  581.5 77.6 %all-reduce.32.cloned.1.call-done = f32[1,64,256]{2,1,0:T(8,128)} async-done(((f32[1,64,256]{2,1,0:T(8,128)}), f32[1,64,256]{2,1,0:T(8,128)}) %all-reduce.32.cloned.1.call-update) | async-done | bytes 65552 | tf_op jit(solution)/shard_map/psum | solution.py:19
  660.1 24.1 %psum.135 = f32[1,64,128]{2,1,0:T(8,128)S(1)} all-reduce(f32[1,64,128]{2,1,0:T(8,128)S(1)} %convolution_bitcast_fusion.1), channel_id=1, replica_groups=mesh['prow'=16,'pcol'=8] {'pcol'}, use_global_device_ids=true, to_apply=%region_19.0 | all-reduce | flops 8192 | bytes 65536 | tf_op jit(solution)/shard_map/psum | solution.py:14
  684.2 1.7 convolution_multiply_fusion.18
  686.0 79.1 %all-reduce.34.cloned.1.call-done = f32[2,64,256]{2,1,0:T(8,128)} async-done(((f32[2,64,256]{2,1,0:T(8,128)}), f32[2,64,256]{2,1,0:T(8,128)}) %all-reduce.34.cloned.1.call-update) | async-done | bytes 131088 | tf_op jit(solution)/shard_map/psum | solution.py:19
  765.1 1.8 fusion.55
  767.0 58.9 %all-reduce.36.cloned.1.call-done = f32[2,64,128]{2,1,0:T(8,128)} async-done(((f32[2,64,128]{2,1,0:T(8,128)}), f32[2,64,128]{2,1,0:T(8,128)}) %all-reduce.36.cloned.1.call-update) | async-done | bytes 65552 | tf_op jit(solution)/shard_map/psum | solution.py:14
  828.0 1.8 fusion.6
  829.9 83.5 %all-reduce.38.cloned.1.call-done = f32[4,64,256]{2,1,0:T(8,128)} async-done(((f32[4,64,256]{2,1,0:T(8,128)}), f32[4,64,256]{2,1,0:T(8,128)}) %all-reduce.38.cloned.1.call-update) | async-done | bytes 262160 | tf_op jit(solution)/shard_map/psum | solution.py:19
  913.4 1.9 fusion.43
  915.3 59.3 %all-reduce.40.cloned.1.call-done = f32[4,64,128]{2,1,0:T(8,128)} async-done(((f32[4,64,128]{2,1,0:T(8,128)}), f32[4,64,128]{2,1,0:T(8,128)}) %all-reduce.40.cloned.1.call-update) | async-done | bytes 131088 | tf_op jit(solution)/shard_map/psum | solution.py:14
  978.3 2.1 fusion.3
  980.4 84.4 %all-reduce.42.cloned.1.call-done = f32[8,64,256]{2,1,0:T(8,128)} async-done(((f32[8,64,256]{2,1,0:T(8,128)}), f32[8,64,256]{2,1,0:T(8,128)}) %all-reduce.42.cloned.1.call-update) | async-done | bytes 524304 | tf_op jit(solution)/shard_map/psum | solution.py:19
  1064.9 2.1 fusion.29
  1067.0 59.7 %all-reduce.44.cloned.1.call-done = f32[8,64,128]{2,1,0:T(8,128)} async-done(((f32[8,64,128]{2,1,0:T(8,128)}), f32[8,64,128]{2,1,0:T(8,128)}) %all-reduce.44.cloned.1.call-update) | async-done | bytes 262160 | tf_op jit(solution)/shard_map/psum | solution.py:14
  1133.6 2.5 fusion
  1138.3 84.3 %all-reduce.46.cloned.1.call-done = f32[16,64,256]{2,1,0:T(8,128)} async-done(((f32[16,64,256]{2,1,0:T(8,128)}), f32[16,64,256]{2,1,0:T(8,128)}) %all-reduce.46.cloned.1.call-update) | async-done | bytes 1048592 | tf_op jit(solution)/shard_map/psum | solution.py:19
  1222.5 2.7 fusion.18
  1227.1 58.2 %all-reduce.48.cloned.1.call-done = f32[16,64,128]{2,1,0:T(8,128)} async-done(((f32[16,64,128]{2,1,0:T(8,128)}), f32[16,64,128]{2,1,0:T(8,128)}) %all-reduce.48.cloned.1.call-update) | async-done | bytes 524304 | tf_op jit(solution)/shard_map/psum | solution.py:14
  (104 shorter events, 38.2 us)
Async XLA Ops:
  7.2 3.0 copy-start.8
  7.2 94.3 %all-reduce.18.cloned.1.call-start = ((), (), s32[]{:S(2)}) async-start(), calls=%async_computation | async-start | bytes 2097152 | tf_op jit(solution)/shard_map/psum | solution.py:19
  10.1 159.7 %all-reduce.20.cloned.1.call-start = ((), (), s32[]{:S(2)}) async-start(), calls=%async_computation.1 | async-start | bytes 524288 | tf_op jit(solution)/shard_map/psum | solution.py:14
  110.6 147.7 %all-reduce.22.cloned.1.call-start = ((), (), s32[]{:S(2)}) async-start(), calls=%async_computation.2 | async-start | bytes 1048576 | tf_op jit(solution)/shard_map/psum | solution.py:19
  172.1 148.9 %all-reduce.24.cloned.1.call-start = ((), (), s32[]{:S(2)}) async-start(), calls=%async_computation.3 | async-start | bytes 262144 | tf_op jit(solution)/shard_map/psum | solution.py:14
  258.3 152.0 %copy-start = (f32[8,64,256]{2,1,0:T(8,128)S(1)}, f32[8,64,256]{2,1,0:T(8,128)}, u32[]{:S(2)}) copy-start(f32[8,64,256]{2,1,0:T(8,128)} %all-reduce.22.cloned.1.call-done) | copy-start | bytes 1572868
  262.2 146.0 %all-reduce.26.cloned.1.call-start = ((), (), s32[]{:S(2)}) async-start(), calls=%async_computation.4 | async-start | bytes 524288 | tf_op jit(solution)/shard_map/psum | solution.py:19
  323.0 146.1 %all-reduce.28.cloned.1.call-start = ((), (), s32[]{:S(2)}) async-start(), calls=%async_computation.5 | async-start | bytes 131072 | tf_op jit(solution)/shard_map/psum | solution.py:14
  408.3 505.1 %copy-start.2 = (f32[4,64,256]{2,1,0:T(8,128)S(1)}, f32[4,64,256]{2,1,0:T(8,128)}, u32[]{:S(2)}) copy-start(f32[4,64,256]{2,1,0:T(8,128)} %all-reduce.26.cloned.1.call-done) | copy-start | bytes 786436
  410.2 144.3 %all-reduce.30.cloned.1.call-start = ((), (), s32[]{:S(2)}) async-start(), calls=%async_computation.6 | async-start | bytes 262144 | tf_op jit(solution)/shard_map/psum | solution.py:19
  470.9 188.2 %all-reduce.32.cloned.1.call-start = ((), (), s32[]{:S(2)}) async-start(), calls=%async_computation.7 | async-start | bytes 131072 | tf_op jit(solution)/shard_map/psum | solution.py:19
  581.5 183.6 %all-reduce.34.cloned.1.call-start = ((), (), s32[]{:S(2)}) async-start(), calls=%async_computation.8 | async-start | bytes 262144 | tf_op jit(solution)/shard_map/psum | solution.py:19
  685.9 140.0 %all-reduce.36.cloned.1.call-start = ((), (), s32[]{:S(2)}) async-start(), calls=%async_computation.9 | async-start | bytes 131072 | tf_op jit(solution)/shard_map/psum | solution.py:14
  767.0 146.4 %all-reduce.38.cloned.1.call-start = ((), (), s32[]{:S(2)}) async-start(), calls=%async_computation.10 | async-start | bytes 524288 | tf_op jit(solution)/shard_map/psum | solution.py:19
  829.9 144.8 %all-reduce.40.cloned.1.call-start = ((), (), s32[]{:S(2)}) async-start(), calls=%async_computation.11 | async-start | bytes 262144 | tf_op jit(solution)/shard_map/psum | solution.py:14
  915.3 149.6 %all-reduce.42.cloned.1.call-start = ((), (), s32[]{:S(2)}) async-start(), calls=%async_computation.12 | async-start | bytes 1048576 | tf_op jit(solution)/shard_map/psum | solution.py:19
  980.4 146.4 %all-reduce.44.cloned.1.call-start = ((), (), s32[]{:S(2)}) async-start(), calls=%async_computation.13 | async-start | bytes 524288 | tf_op jit(solution)/shard_map/psum | solution.py:14
  1067.0 155.5 %all-reduce.46.cloned.1.call-start = ((), (), s32[]{:S(2)}) async-start(), calls=%async_computation.14 | async-start | bytes 2097152 | tf_op jit(solution)/shard_map/psum | solution.py:19
  1127.8 1.0 copy-start.5
  1128.8 7.5 copy-start.4
  1130.3 6.5 copy-start.3
  1130.3 92.2 %copy-start.1 = (f32[16,64,256]{2,1,0:T(8,128)S(1)}, f32[16,64,256]{2,1,0:T(8,128)}, u32[]{:S(2)}) copy-start(f32[16,64,256]{2,1,0:T(8,128)} %all-reduce.18.cloned.1.call-done) | copy-start | bytes 3145732
  1136.2 149.1 %copy-start.6 = (f32[31,64,128]{2,1,0:T(8,128)S(1)}, f32[31,64,128]{2,1,0:T(8,128)}, u32[]{:S(2)}) copy-start(f32[31,64,128]{2,1,0:T(8,128)} %copy-done.5) | copy-start | bytes 3047428
  1136.2 149.1 %all-reduce.48.cloned.1.call-start = ((), (), s32[]{:S(2)}) async-start(), calls=%async_computation.15 | async-start | bytes 1048576 | tf_op jit(solution)/shard_map/psum | solution.py:14
  1286.4 1.0 copy-start.7
Sparse Core Ops, SparseCore 0:
  11.8 89.5 all-reduce.17
  110.7 59.0 all-reduce.19
  173.9 84.3 all-reduce.21
  262.4 58.5 all-reduce.23
  324.9 83.3 all-reduce.25
  411.0 57.9 all-reduce.27
  473.2 81.3 all-reduce.29
  581.6 77.4 all-reduce.31
  686.0 79.0 all-reduce.33
  767.8 58.0 all-reduce.35
  830.0 83.3 all-reduce.37
  916.1 58.4 all-reduce.39
  980.5 84.3 all-reduce.41
  1067.6 59.0 all-reduce.43
  1136.3 86.1 all-reduce.45
  1225.3 59.8 all-reduce.47
where the time goes:
time: 1300 us; the launch traced here: 1290 us
  waiting for transfers between devices  1160 us (89%)
  matrix products  51.5 us (4%)
  blocking collectives  48.1 us (4%)
  between operations  14.3 us (1%)
    psum x9, waiting for transfers between devices, sum_rows(): result = lax.psum(values, 'prow')  753 us
    psum x7, waiting for transfers between devices, sum_columns(): result = lax.psum(values, 'pcol')  411 us
    psum x2, blocking collectives, sum_columns(): result = lax.psum(values, 'pcol')  48.1 us
  transfers between devices with their start and end apart: 16, of which 16 were waited for; matrix products, arithmetic and copies ran while one was open for 1% of the time, Pallas kernels for 0%

commit v1 on v0

--- a/solution.py
+++ b/solution.py
@@ -16,7 +16,7 @@
 
 
 def sum_rows(values):
-    result = lax.psum(values, "prow")
+    result = jnp.sum(lax.all_gather(values, "prow"), axis=0)
     return lax.optimization_barrier(result)
 
 

time: 1300 us -> 1170 us (0.900)
  waiting for transfers between devices: 1160 us -> 1000 us
  other arithmetic: 5.02 us -> 39.8 us
    psum x9 -> x0, waiting for transfers between devices: 753 us -> none  [sum_rows(): result = lax.psum(values, 'prow')]
    all_gather x0 -> x9, waiting for transfers between devices: none -> 590 us  [sum_rows(): result = jnp.sum(lax.all_gather(values, 'prow'), axis=0)]
    reduce_sum x0 -> x9, other arithmetic: none -> 32.6 us  [sum_rows(): result = jnp.sum(lax.all_gather(values, 'prow'), axis=0)]
where the time goes in v1:
time: 1170 us
  waiting for transfers between devices  1000 us (85%)
  matrix products  50.1 us (4%)
  blocking collectives  48.7 us (4%)
  other arithmetic  39.8 us (3%)
  between operations  14.2 us (1%)
    all_gather x9, waiting for transfers between devices, sum_rows(): result = jnp.sum(lax.all_gather(values, 'prow'), axis=0)  590 us
    psum x7, waiting for transfers between devices, sum_columns(): result = lax.psum(values, 'pcol')  412 us
    psum x2, blocking collectives, sum_columns(): result = lax.psum(values, 'pcol')  48.7 us
    reduce_sum x9, other arithmetic, sum_rows(): result = jnp.sum(lax.all_gather(values, 'prow'), axis=0)  32.6 us
  transfers between devices with their start and end apart: 16, of which 16 were waited for; matrix products, arithmetic and copies ran while one was open for 1% of the time, Pallas kernels for 0%

profile of v1, /device:TPU:0, one launch (start us, length us, event | category | flops | bytes accessed | tf_op | source)
XLA Modules:
  0.0 1165.0 jit_solution(1185959574398235363)
XLA Ops:
  7.2 2.8 fusion.20
  10.5 114.2 %all-gather.19.cloned.1.call-done = f32[256,64,256]{2,1,0:T(8,128)} async-done(((f32[16,64,256]{2,1,0:T(8,128)}), f32[256,64,256]{2,1,0:T(8,128)}) %all-gather.19.cloned.1.call-update) | async-done | bytes 16777232 | tf_op jit(solution)/shard_map/all_gather | solution.py:19
  124.7 7.4 reduce_sum.173
  140.1 59.5 %all-reduce.9.cloned.1.call-done = f32[8,64,128]{2,1,0:T(8,128)} async-done(((f32[8,64,128]{2,1,0:T(8,128)}), f32[8,64,128]{2,1,0:T(8,128)}) %all-reduce.9.cloned.1.call-update) | async-done | bytes 262160 | tf_op jit(solution)/shard_map/psum | solution.py:14
  199.6 2.3 fusion.31
  202.3 70.2 %all-gather.21.cloned.1.call-done = f32[128,64,256]{2,1,0:T(8,128)} async-done(((f32[8,64,256]{2,1,0:T(8,128)}), f32[128,64,256]{2,1,0:T(8,128)}) %all-gather.21.cloned.1.call-update) | async-done | bytes 8388624 | tf_op jit(solution)/shard_map/all_gather | solution.py:19
  272.5 4.0 reduce_sum.178
  281.1 58.9 %all-reduce.11.cloned.1.call-done = f32[4,64,128]{2,1,0:T(8,128)} async-done(((f32[4,64,128]{2,1,0:T(8,128)}), f32[4,64,128]{2,1,0:T(8,128)}) %all-reduce.11.cloned.1.call-update) | async-done | bytes 131088 | tf_op jit(solution)/shard_map/psum | solution.py:14
  340.0 2.0 fusion.45
  342.4 50.9 %all-gather.23.cloned.1.call-done = f32[64,64,256]{2,1,0:T(8,128)} async-done(((f32[4,64,256]{2,1,0:T(8,128)}), f32[64,64,256]{2,1,0:T(8,128)}) %all-gather.23.cloned.1.call-update) | async-done | bytes 4194320 | tf_op jit(solution)/shard_map/all_gather | solution.py:19
  393.3 2.5 reduce_sum.182
  397.7 58.4 %all-reduce.13.cloned.1.call-done = f32[2,64,128]{2,1,0:T(8,128)} async-done(((f32[2,64,128]{2,1,0:T(8,128)}), f32[2,64,128]{2,1,0:T(8,128)}) %all-reduce.13.cloned.1.call-update) | async-done | bytes 65552 | tf_op jit(solution)/shard_map/psum | solution.py:14
  460.5 42.8 %all-gather.25.cloned.1.call-done = f32[32,64,256]{2,1,0:T(8,128)} async-done(((f32[2,64,256]{2,1,0:T(8,128)}), f32[32,64,256]{2,1,0:T(8,128)}) %all-gather.25.cloned.1.call-update) | async-done | bytes 2097168 | tf_op jit(solution)/shard_map/all_gather | solution.py:19
  506.9 24.6 %psum.66 = f32[1,64,128]{2,1,0:T(8,128)S(1)} all-reduce(f32[1,64,128]{2,1,0:T(8,128)S(1)} %fusion.72), channel_id=1, replica_groups=mesh['prow'=16,'pcol'=8] {'pcol'}, use_global_device_ids=true, to_apply=%region_17.0 | all-reduce | flops 8192 | bytes 65536 | tf_op jit(solution)/shard_map/psum | solution.py:14
  533.2 39.8 %all-gather.27.cloned.1.call-done = f32[1024,256]{1,0:T(8,128)} async-done(((f32[64,256]{1,0:T(8,128)}), f32[1024,256]{1,0:T(8,128)}) %all-gather.27.cloned.1.call-update) | async-done | bytes 1048592 | tf_op jit(solution)/shard_map/all_gather | solution.py:19
  575.2 24.1 %psum.67 = f32[1,64,128]{2,1,0:T(8,128)S(1)} all-reduce(f32[1,64,128]{2,1,0:T(8,128)S(1)} %convolution_bitcast_fusion), channel_id=1, replica_groups=mesh['prow'=16,'pcol'=8] {'pcol'}, use_global_device_ids=true, to_apply=%region_19.0 | all-reduce | flops 8192 | bytes 65536 | tf_op jit(solution)/shard_map/psum | solution.py:14
  601.7 42.5 %all-gather.29.cloned.1.call-done = f32[32,64,256]{2,1,0:T(8,128)} async-done(((f32[2,64,256]{2,1,0:T(8,128)}), f32[32,64,256]{2,1,0:T(8,128)}) %all-gather.29.cloned.1.call-update) | async-done | bytes 2097168 | tf_op jit(solution)/shard_map/all_gather | solution.py:19
  647.7 58.1 %all-reduce.15.cloned.1.call-done = f32[2,64,128]{2,1,0:T(8,128)} async-done(((f32[2,64,128]{2,1,0:T(8,128)}), f32[2,64,128]{2,1,0:T(8,128)}) %all-reduce.15.cloned.1.call-update) | async-done | bytes 65552 | tf_op jit(solution)/shard_map/psum | solution.py:14
  710.4 50.7 %all-gather.31.cloned.1.call-done = f32[64,64,256]{2,1,0:T(8,128)} async-done(((f32[4,64,256]{2,1,0:T(8,128)}), f32[64,64,256]{2,1,0:T(8,128)}) %all-gather.31.cloned.1.call-update) | async-done | bytes 4194320 | tf_op jit(solution)/shard_map/all_gather | solution.py:19
  761.2 2.5 reduce_sum.190
  765.5 58.9 %all-reduce.17.cloned.1.call-done = f32[4,64,128]{2,1,0:T(8,128)} async-done(((f32[4,64,128]{2,1,0:T(8,128)}), f32[4,64,128]{2,1,0:T(8,128)}) %all-reduce.17.cloned.1.call-update) | async-done | bytes 131088 | tf_op jit(solution)/shard_map/psum | solution.py:14
  828.7 2.1 fusion.3
  830.8 70.0 %all-gather.33.cloned.1.call-done = f32[128,64,256]{2,1,0:T(8,128)} async-done(((f32[8,64,256]{2,1,0:T(8,128)}), f32[128,64,256]{2,1,0:T(8,128)}) %all-gather.33.cloned.1.call-update) | async-done | bytes 8388624 | tf_op jit(solution)/shard_map/all_gather | solution.py:19
  900.8 4.0 reduce_sum.191
  904.8 2.0 fusion.29
  906.9 59.5 %all-reduce.19.cloned.1.call-done = f32[8,64,128]{2,1,0:T(8,128)} async-done(((f32[8,64,128]{2,1,0:T(8,128)}), f32[8,64,128]{2,1,0:T(8,128)}) %all-reduce.19.cloned.1.call-update) | async-done | bytes 262160 | tf_op jit(solution)/shard_map/psum | solution.py:14
  973.0 2.5 fusion
  977.6 108.7 %all-gather.35.cloned.1.call-done = f32[256,64,256]{2,1,0:T(8,128)} async-done(((f32[16,64,256]{2,1,0:T(8,128)}), f32[256,64,256]{2,1,0:T(8,128)}) %all-gather.35.cloned.1.call-update) | async-done | bytes 16777232 | tf_op jit(solution)/shard_map/all_gather | solution.py:19
  1086.3 7.4 reduce_sum.192
  1093.7 2.4 fusion.18
  1098.0 58.6 %all-reduce.21.cloned.1.call-done = f32[16,64,128]{2,1,0:T(8,128)} async-done(((f32[16,64,128]{2,1,0:T(8,128)}), f32[16,64,128]{2,1,0:T(8,128)}) %all-reduce.21.cloned.1.call-update) | async-done | bytes 524304 | tf_op jit(solution)/shard_map/psum | solution.py:14
  1156.6 1.9 constant_dynamic-update-slice_fusion
  (99 shorter events, 54.6 us)
Async XLA Ops:
  7.2 3.0 copy-start.1
  7.2 117.5 %all-gather.19.cloned.1.call-start = ((), (), s32[]{:S(2)}) async-start(), calls=%async_computation.7 | async-start | bytes 17825792 | tf_op jit(solution)/shard_map/all_gather | solution.py:19
  10.1 189.5 %all-reduce.9.cloned.1.call-start = ((), (), s32[]{:S(2)}) async-start(), calls=%async_computation | async-start | bytes 524288 | tf_op jit(solution)/shard_map/psum | solution.py:14
  140.0 132.5 %all-gather.21.cloned.1.call-start = ((), (), s32[]{:S(2)}) async-start(), calls=%async_computation.8 | async-start | bytes 8912896 | tf_op jit(solution)/shard_map/all_gather | solution.py:19
  201.9 138.1 %all-reduce.11.cloned.1.call-start = ((), (), s32[]{:S(2)}) async-start(), calls=%async_computation.1 | async-start | bytes 262144 | tf_op jit(solution)/shard_map/psum | solution.py:14
  279.4 1.0 copy-start
  281.0 112.3 %all-gather.23.cloned.1.call-start = ((), (), s32[]{:S(2)}) async-start(), calls=%async_computation.9 | async-start | bytes 4456448 | tf_op jit(solution)/shard_map/all_gather | solution.py:19
  342.0 114.1 %all-reduce.13.cloned.1.call-start = ((), (), s32[]{:S(2)}) async-start(), calls=%async_computation.2 | async-start | bytes 131072 | tf_op jit(solution)/shard_map/psum | solution.py:14
  397.6 105.7 %all-gather.25.cloned.1.call-start = ((), (), s32[]{:S(2)}) async-start(), calls=%async_computation.10 | async-start | bytes 2228224 | tf_op jit(solution)/shard_map/all_gather | solution.py:19
  457.9 115.0 %all-gather.27.cloned.1.call-start = ((), (), s32[]{:S(2)}) async-start(), calls=%async_computation.11 | async-start | bytes 1114112 | tf_op jit(solution)/shard_map/all_gather | solution.py:19
  533.1 111.1 %all-gather.29.cloned.1.call-start = ((), (), s32[]{:S(2)}) async-start(), calls=%async_computation.12 | async-start | bytes 2228224 | tf_op jit(solution)/shard_map/all_gather | solution.py:19
  601.7 104.1 %all-reduce.15.cloned.1.call-start = ((), (), s32[]{:S(2)}) async-start(), calls=%async_computation.3 | async-start | bytes 131072 | tf_op jit(solution)/shard_map/psum | solution.py:14
  647.7 113.5 %all-gather.31.cloned.1.call-start = ((), (), s32[]{:S(2)}) async-start(), calls=%async_computation.13 | async-start | bytes 4456448 | tf_op jit(solution)/shard_map/all_gather | solution.py:19
  710.4 114.1 %all-reduce.17.cloned.1.call-start = ((), (), s32[]{:S(2)}) async-start(), calls=%async_computation.4 | async-start | bytes 262144 | tf_op jit(solution)/shard_map/psum | solution.py:14
  765.5 135.3 %all-gather.33.cloned.1.call-start = ((), (), s32[]{:S(2)}) async-start(), calls=%async_computation.14 | async-start | bytes 8912896 | tf_op jit(solution)/shard_map/all_gather | solution.py:19
  830.8 135.6 %all-reduce.19.cloned.1.call-start = ((), (), s32[]{:S(2)}) async-start(), calls=%async_computation.5 | async-start | bytes 524288 | tf_op jit(solution)/shard_map/psum | solution.py:14
  906.8 179.4 %all-gather.35.cloned.1.call-start = ((), (), s32[]{:S(2)}) async-start(), calls=%async_computation.15 | async-start | bytes 17825792 | tf_op jit(solution)/shard_map/all_gather | solution.py:19
  975.5 181.1 %all-reduce.21.cloned.1.call-start = ((), (), s32[]{:S(2)}) async-start(), calls=%async_computation.6 | async-start | bytes 1048576 | tf_op jit(solution)/shard_map/psum | solution.py:14
Sparse Core Ops, SparseCore 0:
  10.7 113.9 all-gather.18
  140.1 59.4 all-reduce.8
  202.5 69.9 all-gather.20
  281.2 58.7 all-reduce.10
  342.6 50.6 all-gather.22
  397.8 58.2 all-reduce.12
  459.0 44.2 all-gather.24
  533.2 39.6 all-gather.26
  601.8 42.3 all-gather.28
  647.8 57.9 all-reduce.14
  710.5 50.6 all-gather.30
  765.6 58.7 all-reduce.16
  830.9 69.8 all-gather.32
  907.0 59.4 all-reduce.18
  975.7 110.5 all-gather.34
  1096.2 60.3 all-reduce.20
